TPU v7x, 256 devices: a whole 4x4x8 slice. The times are simulated.
256 devices in a mesh: ia: 16 (over x, z_lo), jb: 16 (over z_hi, y, core).
Axes of the slice: x: 4, y: 4, z: 8 (z_hi: 2, z_lo: 4; z = z_hi * 4 + z_lo), core: 2. Of those that a mesh axis runs over, the one named last changes fastest.
Arguments:
- cycle_w: bfloat16 [16384, 16384], P('ia', 'jb'), may hold values from -0.046875 to 0.046875
- amplitudes: bfloat16 [16384, 4096], P('jb', 'ia'), may hold values from -6 to 6
- fock_vir: float32 [512, 512], replicated, may hold values from -0.25 to 0.25
- energy_i: float32 [32], replicated, may hold values from -2 to -0.5
- energy_j: float32 [8], replicated, may hold values from -2 to -0.5
- energy_vir: float32 [512], replicated, may hold values from 0.3 to 3
Outputs:
- new_amplitudes: float32 [16384, 4096], P('ia', 'jb')
All inputs are finite; a program needn't handle non-finite values.
Results may differ from a plain program's by a relative error of at most 0.0003.
Values may be sent and summed in bfloat16 or wider, within the bound.
A program may use at most 128 MiB of HBM per device.

v0:
```python
import jax
import jax.numpy as jnp
from jax import lax
from jax.sharding import PartitionSpec as P


def from_partner(block, axis, stride):
    count = lax.axis_size(axis)
    route = []
    for low in range(count):
        high = low | 1 << stride
        if high != low and high < count:
            route += [(low, high), (high, low)]
    return lax.ppermute(block, axis, route)


def per_device(cycle_w, amplitudes, fock_vir, energy_i, energy_j, energy_vir):
    highest = lax.Precision.HIGHEST
    partial_value = jnp.dot(
        cycle_w,
        lax.all_gather(amplitudes, "ia", axis=1, tiled=True),
        preferred_element_type=jnp.float32,
    )
    cycle = lax.psum_scatter(partial_value, "jb", scatter_dimension=1, tiled=True)
    row_count = cycle.shape[0]
    half_cols = cycle.shape[1]
    vir_dim = fock_vir.shape[0]
    occ_blocks = row_count // vir_dim
    other = from_partner(cycle, "jb", 0)
    column_index = lax.axis_index("jb")
    parity = column_index % 2
    whole = jnp.where(
        parity == 0,
        jnp.concatenate([cycle, other], axis=1),
        jnp.concatenate([other, cycle], axis=1),
    )
    fock_rows = lax.dynamic_slice_in_dim(fock_vir, parity * half_cols, half_cols, 0)
    blocks = cycle.reshape(occ_blocks, vir_dim, half_cols)
    left = jnp.einsum("ac,icb->iab", fock_vir, blocks, precision=highest)
    right = lax.dot_general(
        whole,
        fock_rows,
        (((1,), (1,)), ((), ())),
        precision=highest,
        preferred_element_type=jnp.float32,
    )
    dressed = blocks + left + right.reshape(occ_blocks, vir_dim, half_cols)
    occ_values = lax.dynamic_slice_in_dim(
        energy_i, lax.axis_index("ia") * occ_blocks, occ_blocks, 0
    )
    pair_value = lax.dynamic_index_in_dim(energy_j, column_index // 2, 0, keepdims=False)
    vir_cols = lax.dynamic_slice_in_dim(energy_vir, parity * half_cols, half_cols, 0)
    denom = (
        occ_values[:, None, None] + pair_value - energy_vir[None, :, None] - vir_cols[None, None, :]
    )
    return (dressed / denom).reshape(row_count, half_cols)


def solution(mesh):
    in_specs = (P("ia", "jb"), P("jb", "ia"), P(), P(), P(), P())
    out_specs = P("ia", "jb")
    return jax.shard_map(
        per_device, mesh=mesh, in_specs=in_specs, out_specs=out_specs, check_vma=False
    )
```

profile of v0, /device:TPU:193, one launch (start us, length us, event | category | flops | bytes accessed | tf_op | source)
XLA Modules:
  0.0 451.4 jit_solution(5551735824897480478)
XLA Ops:
  6.5 0.0 copy-start
  6.5 0.0 all-gather.2.cloned.1.call-start
  6.5 0.7 all-gather.2.cloned.1.call-update
  7.3 0.0 reduce-scatter.2.cloned.1.call-start
  7.3 184.0 %all-gather.2.cloned.1.call-done = bf16[1024,4096]{1,0:T(8,128)(2,1)} async-done(((bf16[1024,256]{1,0:T(8,128)(2,1)}), bf16[1024,4096]{1,0:T(8,128)(2,1)}) %all-gather.2.cloned.1.call-update) | async-done | bytes 8388624 | tf_op jit(solution)/shard_map/all_gather | solution.py:21
  191.3 0.0 copy-done
  191.3 14.5 %fusion.12 = f32[1024,4096]{1,0:T(8,128)} fusion(bf16[1024,1024]{1,0:T(8,128)(2,1)S(1)} %copy-done, bf16[1024,4096]{1,0:T(8,128)(2,1)} %all-gather.2.cloned.1.call-done), kind=kOutput, calls=%fused_computation.17 | convolution fusion | flops 8589934592 | bytes 27262976 | tf_op jit(solution)/shard_map/dot_general | solution.py:19
  205.8 0.0 copy-start.3
  205.8 0.0 copy-start.5
  205.8 0.0 copy-start.4
  205.8 0.0 reduce-scatter.2.cloned.1.call-update
  205.9 216.5 %reduce-scatter.2.cloned.1.call-done = f32[1024,256]{1,0:T(8,128)} async-done(((f32[1024,4096]{1,0:T(8,128)}), f32[1024,256]{1,0:T(8,128)}) %reduce-scatter.2.cloned.1.call-update) | async-done | bytes 1048592 | tf_op jit(solution)/shard_map/reduce_scatter | solution.py:24
  422.3 0.0 copy-start.1
  422.3 1.2 collective-permute-start
  423.6 0.0 copy-done.3
  423.6 0.1 dynamic_slice.16
  423.6 0.0 copy-done.5
  423.6 0.6 dynamic_slice.15
  424.2 0.0 copy-done.4
  424.2 0.7 dynamic-slice_add_fusion
  424.9 0.1 broadcast_subtract_fusion
  425.0 2.5 copy.10
  427.6 0.0 copy-done.1
  427.6 0.0 copy-start.2
  427.6 6.1 %fusion.6 = f32[2,512,256]{1,2,0:T(8,128)} fusion(f32[2,512,256]{1,2,0:T(8,128)} %copy.10, f32[2,512,256]{2,1,0:T(8,128)S(1)} %bitcast.15, f32[512,512]{1,0:T(8,128)} %param.8), kind=kOutput, calls=%fused_computation.8 | convolution fusion | flops 1610874880 | bytes 4194304 | tf_op jit(solution)/shard_map/ac,icb->iab/dot_general | solution.py:39
  433.6 0.0 collective-permute-done
  433.6 0.0 copy-done.2
  433.6 4.4 fusion
  438.0 1.6 copy.11
  439.6 2.4 subtract_divide_fusion
  442.0 2.5 copy.12
Async XLA Ops:
  6.5 184.8 %copy-start = (bf16[1024,1024]{1,0:T(8,128)(2,1)S(1)}, bf16[1024,1024]{1,0:T(8,128)(2,1)}, u32[]{:S(2)}) copy-start(bf16[1024,1024]{1,0:T(8,128)(2,1)} %param.6) | copy-start | bytes 6291460
  6.5 184.8 %all-gather.2.cloned.1.call-start = ((), (), s32[]{:S(2)}) async-start(), calls=%async_computation.1 | async-start | bytes 8912896 | tf_op jit(solution)/shard_map/all_gather | solution.py:21
  7.3 415.1 %reduce-scatter.2.cloned.1.call-start = ((), (), s32[]{:S(2)}) async-start(), calls=%async_computation.2 | async-start | bytes 17825792 | tf_op jit(solution)/shard_map/reduce_scatter | solution.py:24
  205.8 217.7 %copy-start.3 = (f32[512]{0:T(512)S(1)}, f32[512]{0:T(512)}, u32[]{:S(2)}) copy-start(f32[512]{0:T(512)} %param.11) | copy-start | bytes 6148
  205.8 217.8 %copy-start.5 = (f32[8]{0:T(128)S(1)}, f32[8]{0:T(128)}, u32[]{:S(2)}) copy-start(f32[8]{0:T(128)} %param.10) | copy-start | bytes 100
  205.8 218.4 %copy-start.4 = (f32[32]{0:T(128)S(1)}, f32[32]{0:T(128)}, u32[]{:S(2)}) copy-start(f32[32]{0:T(128)} %param.9) | copy-start | bytes 388
  422.3 5.2 %copy-start.1 = (f32[1024,256]{1,0:T(8,128)S(1)}, f32[1024,256]{1,0:T(8,128)}, u32[]{:S(2)}) copy-start(f32[1024,256]{1,0:T(8,128)} %reduce-scatter.2.cloned.1.call-done) | copy-start | bytes 3145732
  422.3 11.3 %collective-permute-start = (f32[1024,256]{1,0:T(8,128)}, f32[1024,256]{1,0:T(8,128)}, u32[]{:S(2)}, u32[]{:S(2)}) collective-permute-start(f32[1024,256]{1,0:T(8,128)} %reduce-scatter.2.cloned.1.call-done), channel_id=1, source_target_pairs={{0,1},{1,0},{2,3},{3,2},{4,5},{5,4},{6,7},{7,6},{8,9},{9,8},{10,11... | collective-permute-start | bytes 3145736 | tf_op jit(solution)/shard_map/ppermute | solution.py:14
  427.6 6.1 %copy-start.2 = (f32[512,512]{1,0:T(8,128)S(1)}, f32[512,512]{1,0:T(8,128)}, u32[]{:S(2)}) copy-start(f32[512,512]{1,0:T(8,128)} %param.8) | copy-start | bytes 3145732
Sparse Core Ops, SparseCore 0:
  9.0 182.2 all-gather.1
  206.0 216.2 reduce-scatter.1
where the time goes:
time: 457 us; the launch traced here: 451 us
  waiting for transfers between devices  401 us (88%)
  matrix products  25 us (5%)
  between operations  13.4 us (3%)
  local copies, waits for them, and re-layouts  7.29 us (2%)
    reduce_scatter x1, waiting for transfers between devices, per_device(): lax.psum_scatter(partial_value, 'jb', scatter_dimension=1, tiled=True)  216 us
    all_gather x1, waiting for transfers between devices, per_device(): lax.all_gather(amplitudes, 'ia', axis=1, tiled=True)  184 us
    dot_general x1, matrix products, per_device(): jnp.dot(cycle_w, lax.all_gather(amplitudes, 'ia', axis=1, tiled=True), pr...  14.5 us
  transfers between devices with their start and end apart: 3, of which 2 were waited for; matrix products, arithmetic and copies ran while one was open for 2% of the time, Pallas kernels for 0%

commit v1 on v0

v1 whole, which is shorter than its diff:
```python
import functools

import jax
import jax.numpy as jnp
from jax import lax
from jax.experimental import pallas as pl
from jax.experimental.pallas import tpu as pltpu
from jax.sharding import PartitionSpec as P

F32 = jnp.float32
BF16 = jnp.bfloat16
MESH = pl.DeviceIdType.MESH

UNITS = (
    ((0, 0, 0), (0, 0, 1)),
    ((-1, 0, 0), (1, 0, 1)),
    ((0, 1, 0), (0, 1, 1)),
    ((-1, 0, 1), (1, 0, 0)),
    ((2, 0, 0), (2, 0, 1)),
    ((-1, 1, 0), (1, 1, 1)),
    ((-1, 1, 1), (1, 1, 0)),
    ((2, 1, 0), (2, 1, 1)),
)
EVENTS = len(UNITS)


def div(a, b):
    return lax.div(a, jnp.int32(b))


def rem(a, b):
    return lax.rem(a, jnp.int32(b))


def split(value):
    high = value.astype(BF16)
    return high, (value - high.astype(F32)).astype(BF16)


def dot3(a, b, dims):
    dot = functools.partial(
        lax.dot_general, dimension_numbers=(dims, ((), ())), preferred_element_type=F32
    )
    return dot(a[0], b[0]) + (dot(a[0], b[1]) + dot(a[1], b[0]))


def kernel(
    w_hbm, a_hbm, fock_hbm, ei_ref, ej_ref, ev_ref, out_ref,
    w2, a2, cb, full, half, relay, rz, racc, roth, rec, fock, fhi, flo,
    loc, wx, ax, recv_a, send_x, send_z, r_half, r_full, send_y,
    r_relay, send_r, send_f, r_final, cx,
):
    M, K = w_hbm.shape
    NB = a_hbm.shape[1]
    HB = NB // 2
    V = fock_hbm.shape[0]
    HM = M // 2

    ia = lax.axis_index("ia")
    jb = lax.axis_index("jb")
    x, zl = div(ia, 4), rem(ia, 4)
    zh, y, c = div(jb, 8), rem(div(jb, 2), 4), rem(jb, 2)
    z = zh * 4 + zl
    f = div(zl, 2)
    g = 1 - f
    owner = c == rem(zl, 2)

    def dev(x=x, y=y, z=z, c=c):
        return {"ia": x * 4 + rem(z, 4), "jb": div(z, 4) * 8 + y * 2 + c}

    xp, xm = dev(x=rem(x + 1, 4)), dev(x=rem(x + 3, 4))
    yp, ym = dev(y=rem(y + 1, 4)), dev(y=rem(y + 3, 4))
    zp2, zm2 = dev(z=rem(z + 2, 8)), dev(z=rem(z + 6, 8))
    up, down = dev(z=rem(z + 1, 8)), dev(z=rem(z + 7, 8))
    partner = dev(c=1 - c)
    has_up, has_down = zl < 3, zl > 0

    def remote(src, dst, send, recv, to):
        return pltpu.make_async_remote_copy(
            src_ref=src, dst_ref=dst, send_sem=send, recv_sem=recv,
            device_id=to, device_id_type=MESH,
        )

    krows = pl.ds(pl.multiple_of(c * K, K), K)
    w_local = pltpu.make_async_copy(w_hbm, w2.at[:, krows], loc.at[0])
    a_local = pltpu.make_async_copy(a_hbm, a2.at[0, krows, :], loc.at[1])
    f_local = pltpu.make_async_copy(fock_hbm, fock, loc.at[2])

    @pl.when(owner)
    def _():
        a_local.start()

    w_local.start()
    f_local.start()

    barrier = pltpu.get_barrier_semaphore()
    for to in (partner, xp, xm, yp, ym, zp2, zm2):
        pl.semaphore_signal(barrier, inc=1, device_id=to, device_id_type=MESH)

    @pl.when(has_up)
    def _():
        pl.semaphore_signal(barrier, inc=1, device_id=up, device_id_type=MESH)

    @pl.when(has_down)
    def _():
        pl.semaphore_signal(barrier, inc=1, device_id=down, device_id_type=MESH)

    pl.semaphore_wait(barrier, 7 + has_up.astype(jnp.int32) + has_down.astype(jnp.int32))

    a_swap = remote(a_hbm, a2.at[0, krows, :], ax.at[0], ax.at[1], partner)
    w_swap = remote(w_hbm, w2.at[:, krows], wx.at[0], wx.at[1], partner)

    @pl.when(jnp.logical_not(owner))
    def _():
        a_swap.start()

    w_swap.start()

    def a_unit(ev, j):
        return a2.at[ev, :, pl.ds(j * HB, HB)]

    def a_wait(ev, j):
        remote(a_unit(ev, j), a_unit(ev, j), send_x.at[0, 0], recv_a.at[ev, j], xp).wait_recv()

    def a_send_x(direction, index, src, ev, j):
        return remote(
            src, a_unit(ev, j), send_x.at[direction, index], recv_a.at[ev, j],
            xp if direction == 0 else xm,
        )

    def a_sends_of(blk):
        ev = 2 * blk
        s = f if blk == 0 else g
        origin = 2 * s + c
        zs, xs = [], []
        for h in range(2):
            there = div(zl + 1, 2)
            ev_up = jnp.where(s == there, 0, 2)
            zs.append((
                jnp.logical_and(has_up, zl >= origin),
                remote(a_unit(ev, h), a_unit(ev_up, h), send_z.at[blk, 0, h], recv_a.at[ev_up, h], up),
            ))
            below = div(zl + 1, 2) - 1
            ev_down = jnp.where(s == below, 0, 2)
            zs.append((
                jnp.logical_and(has_down, zl <= origin),
                remote(a_unit(ev, h), a_unit(ev_down, h), send_z.at[blk, 1, h], recv_a.at[ev_down, h], down),
            ))
        near, far = (1, 3) if blk == 0 else (5, 6)
        for direction in range(2):
            for h in range(2):
                order = h if direction == 0 else 1 - h
                xs.append(a_send_x(
                    direction, 3 * blk + order, a_unit(ev, h), near if order == 0 else far, direction,
                ))
        return zs, xs

    def a_forwards(blk):
        ev, to = (1, 4) if blk == 0 else (5, 7)
        return [a_send_x(d, 3 * blk + 2, a_unit(ev, d), to, d) for d in range(2)]

    def get_a(ev):
        if ev in (0, 2):
            zs, xs = a_sends_of(ev // 2)
            if ev == 0:
                @pl.when(owner)
                def _():
                    a_local.wait()
                    remote(a_hbm, a2.at[0, pl.ds(pl.multiple_of((1 - c) * K, K), K), :], ax.at[0], ax.at[1], partner).wait_recv()
            for h in range(2):
                if ev == 0:
                    @pl.when(jnp.logical_not(owner))
                    def _():
                        a_wait(0, h)
                else:
                    a_wait(ev, h)
                for cond, copy in zs[2 * h:2 * h + 2]:
                    @pl.when(cond)
                    def _():
                        copy.start()
                xs[h].start()
            xs[3].start()
            xs[2].start()
            return
        forwards = a_forwards(0) if ev == 1 else a_forwards(1) if ev == 5 else None
        for j in range(2):
            a_wait(ev, j)
            if forwards:
                forwards[j].start()

    def compute(ev):
        def rows(i, _):
            at = pl.ds(pl.multiple_of(i * HM, HM), HM)
            cb[ev, at, :] = jnp.dot(w2[at, :], a2[ev], preferred_element_type=F32)
            return 0

        lax.fori_loop(0, 2, rows, 0)

    def c_part(ev, j, part):
        return cb.at[ev, pl.ds(part * HM, HM), pl.ds(j * HB, HB)]

    def c_send(ev, j, part, dst, recv, to):
        return remote(c_part(ev, j, part), dst, send_y.at[ev, j, part], recv, to)

    def place(ev, j):
        rel, far, h = UNITS[ev][j]
        xb = rem(x + (rel + 4), 4)
        s = g if far else f
        zd = div(xb, 2)
        yd = 2 * rem(xb, 2) + s
        return zd, rem(yd - y + 4, 4), h

    def to_half(ev, j, part, zd, h):
        slot = zd * 4 + part * 2 + h
        return c_send(ev, j, part, half.at[slot], r_half.at[slot], yp if part == 0 else ym)

    def to_full(ev, j, part, zd, h, side):
        slot = zd * 4 + side * 2 + h
        return c_send(
            ev, j, part, full.at[slot, pl.ds(part * HM, HM), :], r_full.at[slot, part],
            yp if side == 0 else ym,
        )

    def y_first(ev):
        for j in range(2):
            zd, r, h = place(ev, j)

            @pl.when(r == 2)
            def _():
                to_half(ev, j, 0, zd, h).start()
                to_half(ev, j, 1, zd, h).start()

            @pl.when(r == 1)
            def _():
                to_full(ev, j, 1, zd, h, 0).start()

            @pl.when(r == 3)
            def _():
                to_full(ev, j, 0, zd, h, 1).start()

    def y_second(ev):
        for j in range(2):
            zd, r, h = place(ev, j)
            for side, part in ((0, 0), (1, 1)):
                @pl.when(r == 1 + 2 * side)
                def _():
                    to_half(ev, j, part, zd, h).wait_recv()
                    slot = zd * 4 + part * 2 + h
                    at = (ev, pl.ds(part * HM, HM), pl.ds(j * HB, HB))
                    cb[at] = cb[at] + half[slot]
                    to_full(ev, j, part, zd, h, side).start()

    def to_relay(ev, j, part, h):
        return remote(
            c_part(ev, j, part), relay.at[part * 2 + h], send_r.at[part * 2 + h],
            r_relay.at[part * 2 + h], zp2 if part == 0 else zm2,
        )

    def y_last(ev):
        for j in range(2):
            zd, r, h = place(ev, j)

            @pl.when(r == 0)
            def _():
                for side in range(2):
                    for part in range(2):
                        to_full(ev, j, part, zd, h, side).wait_recv()
                cols = pl.ds(j * HB, HB)
                total = cb[ev, :, cols] + full[zd * 4 + h] + full[zd * 4 + 2 + h]

                @pl.when(zd == zh)
                def _():
                    racc[:, pl.ds(h * HB, HB)] = total

                @pl.when(zd != zh)
                def _():
                    cb[ev, :, cols] = total
                    to_relay(ev, j, 0, h).start()
                    to_relay(ev, j, 1, h).start()

    def to_final(part, h):
        return remote(
            relay.at[part * 2 + h], rz.at[h, pl.ds(part * HM, HM), :], send_f.at[part * 2 + h],
            r_final.at[part * 2 + h], zp2 if part == 0 else zm2,
        )

    def event_of(source, h):
        xb = 2 * (1 - div(source, 4)) + div(y, 2)
        rel = rem(xb - x + 4, 4)
        isf = rem(y, 2) == div(rem(source, 4), 2)
        near, far = jnp.where(isf, 1, 5), jnp.where(isf, 3, 6)
        side = (near, far) if h == 0 else (far, near)
        own, opposite = jnp.where(isf, 0, 2), jnp.where(isf, 4, 7)
        return jnp.where(
            rel == 0, own, jnp.where(rel == 2, opposite, jnp.where(rel == 3, side[0], side[1]))
        )

    def z_relay(step):
        for part in range(2):
            source = rem(z + (6 if part == 0 else 2), 8)
            for h in range(2):
                @pl.when(event_of(source, h) == step)
                def _():
                    remote(
                        relay.at[part * 2 + h], relay.at[part * 2 + h], send_r.at[part * 2 + h],
                        r_relay.at[part * 2 + h], zp2,
                    ).wait_recv()
                    to_final(part, h).start()

    def prepare():
        f_local.wait()
        fhi[...], flo[...] = split(fock[...])
        levels = jnp.broadcast_to(ev_ref[...], (128, V)).T
        here = ev_ref[:, pl.ds(pl.multiple_of(c * NB, NB), NB)]
        for i in range(M // V):
            pair = ei_ref[ia * (M // V) + i] + ej_ref[div(jb, 2)]
            for k in range(NB // 128):
                cols = pl.ds(k * 128, 128)
                denom = pair - levels - here[:, k * 128:(k + 1) * 128]
                rec[pl.ds(i * V, V), cols] = 1.0 / denom

    for step in range(EVENTS + 4):
        if step < EVENTS:
            get_a(step)
            if step == 0:
                w_local.wait()
                remote(w_hbm, w2.at[:, pl.ds(pl.multiple_of((1 - c) * K, K), K)], wx.at[0], wx.at[1], partner).wait_recv()
            compute(step)
            y_first(step)
            if step == 0:
                prepare()
        if 0 <= step - 1 < EVENTS:
            y_second(step - 1)
        if 0 <= step - 2 < EVENTS:
            y_last(step - 2)
        if 0 <= step - 3 < EVENTS:
            z_relay(step - 3)

    for h in range(2):
        for part in range(2):
            to_final(part, h).wait_recv()
        cols = pl.ds(h * HB, HB)
        racc[:, cols] = racc[:, cols] + rz[h]

    swap = remote(racc, roth, cx.at[0], cx.at[1], partner)
    swap.start()

    mine = pl.ds(pl.multiple_of(c * NB, NB), NB)
    other = pl.ds(pl.multiple_of((1 - c) * NB, NB), NB)
    nn, nt = ((1,), (0,)), ((1,), (1,))
    for i in range(M // V):
        at = pl.ds(i * V, V)
        value = racc[at, :]
        parts = split(value)
        rows = value + dot3((fhi[...], flo[...]), parts, nn)
        out_ref[at, :] = rows + dot3(parts, (fhi[mine, mine], flo[mine, mine]), nt)
    swap.wait_recv()
    for i in range(M // V):
        at = pl.ds(i * V, V)
        parts = split(roth[at, :])
        out_ref[at, :] = (
            out_ref[at, :] + dot3(parts, (fhi[mine, other], flo[mine, other]), nt)
        ) * rec[at, :]

    swap.wait_send()
    w_swap.wait_send()

    @pl.when(jnp.logical_not(owner))
    def _():
        a_swap.wait_send()

    for blk in range(2):
        zs, xs = a_sends_of(blk)
        for cond, copy in zs:
            @pl.when(cond)
            def _():
                copy.wait_send()
        for copy in xs + a_forwards(blk):
            copy.wait_send()
    for ev in range(EVENTS):
        for j in range(2):
            zd, r, h = place(ev, j)

            @pl.when(r != 0)
            def _():
                for part in range(2):
                    to_half(ev, j, part, zd, h).wait_send()
    for part in range(2):
        for h in range(2):
            to_relay(0, 0, part, h).wait_send()
            to_final(part, h).wait_send()


def per_device(cycle_w, amplitudes, fock_vir, energy_i, energy_j, energy_vir):
    M, K = cycle_w.shape
    NB = amplitudes.shape[1]
    HB, HM = NB // 2, M // 2
    V = fock_vir.shape[0]
    dma = pltpu.SemaphoreType.DMA
    anywhere = pl.BlockSpec(memory_space=pl.ANY)
    vmem = pl.BlockSpec(memory_space=pltpu.VMEM)
    smem = pl.BlockSpec(memory_space=pltpu.SMEM)
    return pl.pallas_call(
        kernel,
        out_shape=jax.ShapeDtypeStruct((M, NB), F32),
        in_specs=[anywhere, anywhere, anywhere, smem, smem, vmem],
        out_specs=vmem,
        scratch_shapes=[
            pltpu.VMEM((M, 2 * K), BF16),
            pltpu.VMEM((EVENTS, 2 * K, NB), BF16),
            pltpu.VMEM((EVENTS, M, NB), F32),
            pltpu.VMEM((8, M, HB), F32),
            pltpu.VMEM((8, HM, HB), F32),
            pltpu.VMEM((4, HM, HB), F32),
            pltpu.VMEM((2, M, HB), F32),
            pltpu.VMEM((M, NB), F32),
            pltpu.VMEM((M, NB), F32),
            pltpu.VMEM((M, NB), F32),
            pltpu.VMEM((V, V), F32),
            pltpu.VMEM((V, V), BF16),
            pltpu.VMEM((V, V), BF16),
            dma((3,)), dma((2,)), dma((2,)), dma((EVENTS, 2)), dma((2, 6)), dma((2, 2, 2)),
            dma((8,)), dma((8, 2)), dma((EVENTS, 2, 2)),
            dma((4,)), dma((4,)), dma((4,)), dma((4,)), dma((2,)),
        ],
        compiler_params=pltpu.CompilerParams(
            collective_id=0, has_side_effects=True, vmem_limit_bytes=60 * 1024 * 1024
        ),
        name="residual",
    )(cycle_w, amplitudes, fock_vir, energy_i, energy_j, energy_vir.reshape(1, -1))


def solution(mesh):
    in_specs = (P("ia", "jb"), P("jb", "ia"), P(), P(), P(), P())
    out_specs = P("ia", "jb")
    return jax.shard_map(
        per_device, mesh=mesh, in_specs=in_specs, out_specs=out_specs, check_vma=False
    )
```

time: 457 us -> 204 us (0.45)
  the two profiles are of different devices: /device:TPU:193 before, /device:TPU:119 now
where the time goes in v1:
time: 204 us
  Pallas kernels  202 us (99%)
  local copies, waits for them, and re-layouts  2.26 us (1%)
    pallas_call x1, Pallas kernels, per_device(): pl.pallas_call(kernel, out_shape=jax.ShapeDtypeStruct((M, NB), F32), in_s...  202 us

profile of v1, /device:TPU:119, one launch (start us, length us, event | category | flops | bytes accessed | tf_op | source)
XLA Modules:
  0.0 204.1 jit_solution(17266591425835152390)
XLA Ops:
  0.0 201.9 %residual.1 = f32[1024,256]{1,0:T(8,128)} custom-call(bf16[1024,1024]{1,0:T(8,128)(2,1)} %w_hbm.1, bf16[1024,256]{1,0:T(8,128)(2,1)} %a_hbm.1, f32[512,512]{1,0:T(8,128)} %fock_hbm.1, f32[32]{0:T(128)} %ei_ref.1, f32[8]{0:T(128)} %ej_ref.1, f32[1,512]{1,0:T(1,128)} %bitcast.1), custom_call_target="tpu_custom_call" | custom-call | tf_op jit(solution)/shard_map/residual/pallas_call | solution.py:403
  201.9 2.3 %copy.8 = f32[1024,256]{1,0:T(8,128)} copy(f32[1024,256]{1,0:T(8,128)} %residual.1) | data formatting | bytes 2097152

commit v2 on v1

--- a/solution.py
+++ b/solution.py
@@ -14,14 +14,21 @@
 UNITS = (
     ((0, 0, 0), (0, 0, 1)),
     ((-1, 0, 0), (1, 0, 1)),
+    ((-1, 0, 1), (1, 0, 0)),
     ((0, 1, 0), (0, 1, 1)),
-    ((-1, 0, 1), (1, 0, 0)),
+    ((-1, 1, 0), (1, 1, 1)),
     ((2, 0, 0), (2, 0, 1)),
-    ((-1, 1, 0), (1, 1, 1)),
     ((-1, 1, 1), (1, 1, 0)),
     ((2, 1, 0), (2, 1, 1)),
 )
+OWN, NEAR, FAR, OPPOSITE = (0, 3), (1, 4), (2, 6), (5, 7)
 EVENTS = len(UNITS)
+
+LEVEL = 10
+BASE = 2 * LEVEL + 1
+REST = 2.0 ** -8 / LEVEL
+TINY = 1e-30
+CHUNK = 64
 
 
 def div(a, b):
@@ -46,9 +53,9 @@
 
 def kernel(
     w_hbm, a_hbm, fock_hbm, ei_ref, ej_ref, ev_ref, out_ref,
-    w2, a2, cb, full, half, relay, rz, racc, roth, rec, fock, fhi, flo,
+    w2, a2, cb, sent, full, half, rz, racc, roth, rec, fock, fhi, flo,
     loc, wx, ax, recv_a, send_x, send_z, r_half, r_full, send_y,
-    r_relay, send_r, send_f, r_final, cx,
+    send_f, r_final, cx,
 ):
     M, K = w_hbm.shape
     NB = a_hbm.shape[1]
@@ -70,7 +77,7 @@
 
     xp, xm = dev(x=rem(x + 1, 4)), dev(x=rem(x + 3, 4))
     yp, ym = dev(y=rem(y + 1, 4)), dev(y=rem(y + 3, 4))
-    zp2, zm2 = dev(z=rem(z + 2, 8)), dev(z=rem(z + 6, 8))
+    z4 = dev(z=rem(z + 4, 8))
     up, down = dev(z=rem(z + 1, 8)), dev(z=rem(z + 7, 8))
     partner = dev(c=1 - c)
     has_up, has_down = zl < 3, zl > 0
@@ -94,7 +101,7 @@
     f_local.start()
 
     barrier = pltpu.get_barrier_semaphore()
-    for to in (partner, xp, xm, yp, ym, zp2, zm2):
+    for to in (partner, xp, xm, yp, ym, z4):
         pl.semaphore_signal(barrier, inc=1, device_id=to, device_id_type=MESH)
 
     @pl.when(has_up)
@@ -105,7 +112,7 @@
     def _():
         pl.semaphore_signal(barrier, inc=1, device_id=down, device_id_type=MESH)
 
-    pl.semaphore_wait(barrier, 7 + has_up.astype(jnp.int32) + has_down.astype(jnp.int32))
+    pl.semaphore_wait(barrier, 6 + has_up.astype(jnp.int32) + has_down.astype(jnp.int32))
 
     a_swap = remote(a_hbm, a2.at[0, krows, :], ax.at[0], ax.at[1], partner)
     w_swap = remote(w_hbm, w2.at[:, krows], wx.at[0], wx.at[1], partner)
@@ -129,24 +136,24 @@
         )
 
     def a_sends_of(blk):
-        ev = 2 * blk
+        ev = OWN[blk]
         s = f if blk == 0 else g
         origin = 2 * s + c
         zs, xs = [], []
         for h in range(2):
             there = div(zl + 1, 2)
-            ev_up = jnp.where(s == there, 0, 2)
+            ev_up = jnp.where(s == there, OWN[0], OWN[1])
             zs.append((
                 jnp.logical_and(has_up, zl >= origin),
                 remote(a_unit(ev, h), a_unit(ev_up, h), send_z.at[blk, 0, h], recv_a.at[ev_up, h], up),
             ))
             below = div(zl + 1, 2) - 1
-            ev_down = jnp.where(s == below, 0, 2)
+            ev_down = jnp.where(s == below, OWN[0], OWN[1])
             zs.append((
                 jnp.logical_and(has_down, zl <= origin),
                 remote(a_unit(ev, h), a_unit(ev_down, h), send_z.at[blk, 1, h], recv_a.at[ev_down, h], down),
             ))
-        near, far = (1, 3) if blk == 0 else (5, 6)
+        near, far = NEAR[blk], FAR[blk]
         for direction in range(2):
             for h in range(2):
                 order = h if direction == 0 else 1 - h
@@ -156,12 +163,11 @@
         return zs, xs
 
     def a_forwards(blk):
-        ev, to = (1, 4) if blk == 0 else (5, 7)
-        return [a_send_x(d, 3 * blk + 2, a_unit(ev, d), to, d) for d in range(2)]
+        return [a_send_x(d, 3 * blk + 2, a_unit(NEAR[blk], d), OPPOSITE[blk], d) for d in range(2)]
 
     def get_a(ev):
-        if ev in (0, 2):
-            zs, xs = a_sends_of(ev // 2)
+        if ev in OWN:
+            zs, xs = a_sends_of(OWN.index(ev))
             if ev == 0:
                 @pl.when(owner)
                 def _():
@@ -178,15 +184,25 @@
                     @pl.when(cond)
                     def _():
                         copy.start()
-                xs[h].start()
-            xs[3].start()
-            xs[2].start()
+                if ev == 0:
+                    xs[h].start()
+            if ev == 0:
+                xs[3].start()
+                xs[2].start()
+            else:
+                forwards = a_forwards(0)
+                xs[0].start()
+                xs[3].start()
+                forwards[0].start()
+                forwards[1].start()
+                xs[1].start()
+                xs[2].start()
             return
-        forwards = a_forwards(0) if ev == 1 else a_forwards(1) if ev == 5 else None
         for j in range(2):
             a_wait(ev, j)
-            if forwards:
-                forwards[j].start()
+        if ev == NEAR[1]:
+            for copy in a_forwards(1):
+                copy.start()
 
     def compute(ev):
         def rows(i, _):
@@ -196,11 +212,48 @@
 
         lax.fori_loop(0, 2, rows, 0)
 
-    def c_part(ev, j, part):
-        return cb.at[ev, pl.ds(part * HM, HM), pl.ds(j * HB, HB)]
+    def chunk(i, second):
+        return pl.ds(pl.multiple_of(i * CHUNK + second * (HM // 2), CHUNK), CHUNK)
+
+    def packed(ref, values, i):
+        numbers = []
+        for k in range(2):
+            high = values[k].astype(BF16)
+            near = high.astype(F32)
+            ref[chunk(i, k), :] = high
+            size = jnp.maximum(jnp.abs(near), TINY)
+            numbers.append(jnp.round((values[k] - near) * (pl.reciprocal(size, approx=True) * (1.0 / REST))))
+        ref[chunk(i, 2), :] = (numbers[0] * BASE + numbers[1]).astype(BF16)
+
+    def unpacked(ref, i):
+        both = ref[chunk(i, 2), :].astype(F32)
+        top = jnp.round(both * (1.0 / BASE))
+        numbers = (top, both - top * BASE)
+        values = []
+        for k in range(2):
+            high = ref[chunk(i, k), :].astype(F32)
+            values.append(high + numbers[k] * (jnp.abs(high) * REST))
+        return values
+
+    def c_rows(ev, j, part, i, k):
+        at = pl.ds(pl.multiple_of(part * HM + i * CHUNK + k * (HM // 2), CHUNK), CHUNK)
+        return cb[ev, at, pl.ds(j * HB, HB)]
+
+    def c_sum(ev, j, part, arrived, store):
+        def step(i, _):
+            values = [c_rows(ev, j, part, i, k) for k in range(2)]
+            for ref in arrived:
+                values = [a + b for a, b in zip(values, unpacked(ref, i))]
+            store(i, values)
+            return 0
+
+        lax.fori_loop(0, HM // 2 // CHUNK, step, 0)
+
+    def c_pack(ev, j, part, *arrived):
+        c_sum(ev, j, part, arrived, lambda i, values: packed(sent.at[ev, j, part], values, i))
 
     def c_send(ev, j, part, dst, recv, to):
-        return remote(c_part(ev, j, part), dst, send_y.at[ev, j, part], recv, to)
+        return remote(sent.at[ev, j, part], dst, send_y.at[ev, j, part], recv, to)
 
     def place(ev, j):
         rel, far, h = UNITS[ev][j]
@@ -217,95 +270,67 @@
     def to_full(ev, j, part, zd, h, side):
         slot = zd * 4 + side * 2 + h
         return c_send(
-            ev, j, part, full.at[slot, pl.ds(part * HM, HM), :], r_full.at[slot, part],
+            ev, j, part, full.at[slot, part], r_full.at[slot, part],
             yp if side == 0 else ym,
         )
 
     def y_first(ev):
         for j in range(2):
             zd, r, h = place(ev, j)
-
-            @pl.when(r == 2)
-            def _():
-                to_half(ev, j, 0, zd, h).start()
-                to_half(ev, j, 1, zd, h).start()
-
-            @pl.when(r == 1)
-            def _():
-                to_full(ev, j, 1, zd, h, 0).start()
-
-            @pl.when(r == 3)
-            def _():
-                to_full(ev, j, 0, zd, h, 1).start()
+            for part in range(2):
+                @pl.when(jnp.logical_or(r == 2, r == 3 - 2 * part))
+                def _():
+                    c_pack(ev, j, part)
+
+                @pl.when(r == 2)
+                def _():
+                    to_half(ev, j, part, zd, h).start()
+
+                @pl.when(r == 3 - 2 * part)
+                def _():
+                    to_full(ev, j, part, zd, h, 1 - part).start()
 
     def y_second(ev):
         for j in range(2):
             zd, r, h = place(ev, j)
-            for side, part in ((0, 0), (1, 1)):
-                @pl.when(r == 1 + 2 * side)
+            for part in range(2):
+                @pl.when(r == 1 + 2 * part)
                 def _():
                     to_half(ev, j, part, zd, h).wait_recv()
-                    slot = zd * 4 + part * 2 + h
-                    at = (ev, pl.ds(part * HM, HM), pl.ds(j * HB, HB))
-                    cb[at] = cb[at] + half[slot]
-                    to_full(ev, j, part, zd, h, side).start()
-
-    def to_relay(ev, j, part, h):
+                    c_pack(ev, j, part, half.at[zd * 4 + part * 2 + h])
+                    to_full(ev, j, part, zd, h, part).start()
+
+    def to_other(ev, j, part, h):
         return remote(
-            c_part(ev, j, part), relay.at[part * 2 + h], send_r.at[part * 2 + h],
-            r_relay.at[part * 2 + h], zp2 if part == 0 else zm2,
+            sent.at[ev, j, part], rz.at[h, part], send_f.at[h, part], r_final.at[h, part], z4
         )
 
     def y_last(ev):
         for j in range(2):
             zd, r, h = place(ev, j)
-
-            @pl.when(r == 0)
-            def _():
-                for side in range(2):
-                    for part in range(2):
+            for part in range(2):
+                arrived = [full.at[zd * 4 + side * 2 + h, part] for side in range(2)]
+
+                @pl.when(r == 0)
+                def _():
+                    for side in range(2):
                         to_full(ev, j, part, zd, h, side).wait_recv()
-                cols = pl.ds(j * HB, HB)
-                total = cb[ev, :, cols] + full[zd * 4 + h] + full[zd * 4 + 2 + h]
-
-                @pl.when(zd == zh)
-                def _():
-                    racc[:, pl.ds(h * HB, HB)] = total
-
-                @pl.when(zd != zh)
-                def _():
-                    cb[ev, :, cols] = total
-                    to_relay(ev, j, 0, h).start()
-                    to_relay(ev, j, 1, h).start()
-
-    def to_final(part, h):
-        return remote(
-            relay.at[part * 2 + h], rz.at[h, pl.ds(part * HM, HM), :], send_f.at[part * 2 + h],
-            r_final.at[part * 2 + h], zp2 if part == 0 else zm2,
-        )
-
-    def event_of(source, h):
-        xb = 2 * (1 - div(source, 4)) + div(y, 2)
-        rel = rem(xb - x + 4, 4)
-        isf = rem(y, 2) == div(rem(source, 4), 2)
-        near, far = jnp.where(isf, 1, 5), jnp.where(isf, 3, 6)
-        side = (near, far) if h == 0 else (far, near)
-        own, opposite = jnp.where(isf, 0, 2), jnp.where(isf, 4, 7)
-        return jnp.where(
-            rel == 0, own, jnp.where(rel == 2, opposite, jnp.where(rel == 3, side[0], side[1]))
-        )
-
-    def z_relay(step):
-        for part in range(2):
-            source = rem(z + (6 if part == 0 else 2), 8)
-            for h in range(2):
-                @pl.when(event_of(source, h) == step)
-                def _():
-                    remote(
-                        relay.at[part * 2 + h], relay.at[part * 2 + h], send_r.at[part * 2 + h],
-                        r_relay.at[part * 2 + h], zp2,
-                    ).wait_recv()
-                    to_final(part, h).start()
+
+                def keep(i, values):
+                    for k in range(2):
+                        racc[r_rows(part, i, k), pl.ds(h * HB, HB)] = values[k]
+
+                @pl.when(jnp.logical_and(r == 0, zd == zh))
+                def _():
+                    c_sum(ev, j, part, arrived, keep)
+
+                @pl.when(jnp.logical_and(r == 0, zd != zh))
+                def _():
+                    c_pack(ev, j, part, *arrived)
+                    to_other(ev, j, part, h).start()
+
+    def r_rows(part, i, k):
+        return pl.ds(pl.multiple_of(part * HM + i * CHUNK + k * (HM // 2), CHUNK), CHUNK)
 
     def prepare():
         f_local.wait()
@@ -319,7 +344,9 @@
                 denom = pair - levels - here[:, k * 128:(k + 1) * 128]
                 rec[pl.ds(i * V, V), cols] = 1.0 / denom
 
-    for step in range(EVENTS + 4):
+    L2 = 1
+    L3 = 3
+    for step in range(EVENTS + L3):
         if step < EVENTS:
             get_a(step)
             if step == 0:
@@ -329,18 +356,23 @@
             y_first(step)
             if step == 0:
                 prepare()
-        if 0 <= step - 1 < EVENTS:
-            y_second(step - 1)
-        if 0 <= step - 2 < EVENTS:
-            y_last(step - 2)
-        if 0 <= step - 3 < EVENTS:
-            z_relay(step - 3)
+        if 0 <= step - L2 < EVENTS:
+            y_second(step - L2)
+        if 0 <= step - L3 < EVENTS:
+            y_last(step - L3)
 
     for h in range(2):
         for part in range(2):
-            to_final(part, h).wait_recv()
-        cols = pl.ds(h * HB, HB)
-        racc[:, cols] = racc[:, cols] + rz[h]
+            to_other(0, 0, part, h).wait_recv()
+
+            def finish(i, _):
+                values = unpacked(rz.at[h, part], i)
+                for k in range(2):
+                    at = (r_rows(part, i, k), pl.ds(h * HB, HB))
+                    racc[at] = racc[at] + values[k]
+                return 0
+
+            lax.fori_loop(0, HM // 2 // CHUNK, finish, 0)
 
     swap = remote(racc, roth, cx.at[0], cx.at[1], partner)
     swap.start()
@@ -385,10 +417,9 @@
             def _():
                 for part in range(2):
                     to_half(ev, j, part, zd, h).wait_send()
-    for part in range(2):
-        for h in range(2):
-            to_relay(0, 0, part, h).wait_send()
-            to_final(part, h).wait_send()
+    for h in range(2):
+        for part in range(2):
+            to_other(0, 0, part, h).wait_send()
 
 
 def per_device(cycle_w, amplitudes, fock_vir, energy_i, energy_j, energy_vir):
@@ -409,10 +440,10 @@
             pltpu.VMEM((M, 2 * K), BF16),
             pltpu.VMEM((EVENTS, 2 * K, NB), BF16),
             pltpu.VMEM((EVENTS, M, NB), F32),
-            pltpu.VMEM((8, M, HB), F32),
-            pltpu.VMEM((8, HM, HB), F32),
-            pltpu.VMEM((4, HM, HB), F32),
-            pltpu.VMEM((2, M, HB), F32),
+            pltpu.VMEM((EVENTS, 2, 2, HM * 3 // 2, HB), BF16),
+            pltpu.VMEM((8, 2, HM * 3 // 2, HB), BF16),
+            pltpu.VMEM((8, HM * 3 // 2, HB), BF16),
+            pltpu.VMEM((2, 2, HM * 3 // 2, HB), BF16),
             pltpu.VMEM((M, NB), F32),
             pltpu.VMEM((M, NB), F32),
             pltpu.VMEM((M, NB), F32),
@@ -421,7 +452,7 @@
             pltpu.VMEM((V, V), BF16),
             dma((3,)), dma((2,)), dma((2,)), dma((EVENTS, 2)), dma((2, 6)), dma((2, 2, 2)),
             dma((8,)), dma((8, 2)), dma((EVENTS, 2, 2)),
-            dma((4,)), dma((4,)), dma((4,)), dma((4,)), dma((2,)),
+            dma((2, 2)), dma((2, 2)), dma((2,)),
         ],
         compiler_params=pltpu.CompilerParams(
             collective_id=0, has_side_effects=True, vmem_limit_bytes=60 * 1024 * 1024

time: 204 us -> 136 us (0.67)
  the two profiles are of different devices: /device:TPU:119 before, /device:TPU:193 now
where the time goes in v2:
time: 136 us
  Pallas kernels  133 us (98%)
  local copies, waits for them, and re-layouts  2.26 us (2%)
    pallas_call x1, Pallas kernels, per_device(): pl.pallas_call(kernel, out_shape=jax.ShapeDtypeStruct((M, NB), F32), in_s...  133 us

profile of v2, /device:TPU:193, one launch (start us, length us, event | category | flops | bytes accessed | tf_op | source)
XLA Modules:
  0.0 135.7 jit_solution(9382179060607739414)
XLA Ops:
  0.0 133.4 %residual.1 = f32[1024,256]{1,0:T(8,128)} custom-call(bf16[1024,1024]{1,0:T(8,128)(2,1)} %w_hbm.1, bf16[1024,256]{1,0:T(8,128)(2,1)} %a_hbm.1, f32[512,512]{1,0:T(8,128)} %fock_hbm.1, f32[32]{0:T(128)} %ei_ref.1, f32[8]{0:T(128)} %ej_ref.1, f32[1,512]{1,0:T(1,128)} %bitcast.1), custom_call_target="tpu_custom_call" | custom-call | tf_op jit(solution)/shard_map/residual/pallas_call | solution.py:434
  133.4 2.3 %copy.8 = f32[1024,256]{1,0:T(8,128)} copy(f32[1024,256]{1,0:T(8,128)} %residual.1) | data formatting | bytes 2097152

commit v3 on v2

--- a/solution.py
+++ b/solution.py
@@ -16,12 +16,13 @@
     ((-1, 0, 0), (1, 0, 1)),
     ((-1, 0, 1), (1, 0, 0)),
     ((0, 1, 0), (0, 1, 1)),
+    ((2, 0, 0), (2, 0, 1)),
     ((-1, 1, 0), (1, 1, 1)),
-    ((2, 0, 0), (2, 0, 1)),
     ((-1, 1, 1), (1, 1, 0)),
     ((2, 1, 0), (2, 1, 1)),
 )
-OWN, NEAR, FAR, OPPOSITE = (0, 3), (1, 4), (2, 6), (5, 7)
+OWN, NEAR, FAR, OPPOSITE = (0, 3), (1, 5), (2, 6), (4, 7)
+L2, L3 = 1, 3
 EVENTS = len(UNITS)
 
 LEVEL = 10
@@ -167,14 +168,15 @@
 
     def get_a(ev):
         if ev in OWN:
-            zs, xs = a_sends_of(OWN.index(ev))
-            if ev == 0:
+            blk = OWN.index(ev)
+            zs, xs = a_sends_of(blk)
+            if blk == 0:
                 @pl.when(owner)
                 def _():
                     a_local.wait()
                     remote(a_hbm, a2.at[0, pl.ds(pl.multiple_of((1 - c) * K, K), K), :], ax.at[0], ax.at[1], partner).wait_recv()
             for h in range(2):
-                if ev == 0:
+                if blk == 0:
                     @pl.when(jnp.logical_not(owner))
                     def _():
                         a_wait(0, h)
@@ -184,25 +186,14 @@
                     @pl.when(cond)
                     def _():
                         copy.start()
-                if ev == 0:
-                    xs[h].start()
-            if ev == 0:
-                xs[3].start()
-                xs[2].start()
-            else:
-                forwards = a_forwards(0)
-                xs[0].start()
-                xs[3].start()
-                forwards[0].start()
-                forwards[1].start()
-                xs[1].start()
-                xs[2].start()
+                xs[h].start()
+            xs[3].start()
+            xs[2].start()
             return
         for j in range(2):
             a_wait(ev, j)
-        if ev == NEAR[1]:
-            for copy in a_forwards(1):
-                copy.start()
+            if ev in NEAR:
+                a_forwards(NEAR.index(ev))[j].start()
 
     def compute(ev):
         def rows(i, _):
@@ -344,8 +335,6 @@
                 denom = pair - levels - here[:, k * 128:(k + 1) * 128]
                 rec[pl.ds(i * V, V), cols] = 1.0 / denom
 
-    L2 = 1
-    L3 = 3
     for step in range(EVENTS + L3):
         if step < EVENTS:
             get_a(step)

time: 136 us -> 125 us (0.919)
  Pallas kernels: 133 us -> 122 us
    pallas_call x1, Pallas kernels: 133 us -> 122 us  [per_device(): pl.pallas_call(kernel, out_shape=jax.ShapeDtypeStruct((M, NB), F32), in_s...]
where the time goes in v3:
time: 125 us; the launch traced here: 124 us
  Pallas kernels  122 us (98%)
  local copies, waits for them, and re-layouts  2.26 us (2%)
    pallas_call x1, Pallas kernels, per_device(): pl.pallas_call(kernel, out_shape=jax.ShapeDtypeStruct((M, NB), F32), in_s...  122 us

profile of v3, /device:TPU:193, one launch (start us, length us, event | category | flops | bytes accessed | tf_op | source)
XLA Modules:
  0.0 124.4 jit_solution(9223005628017577891)
XLA Ops:
  0.0 122.1 %residual.1 = f32[1024,256]{1,0:T(8,128)} custom-call(bf16[1024,1024]{1,0:T(8,128)(2,1)} %w_hbm.1, bf16[1024,256]{1,0:T(8,128)(2,1)} %a_hbm.1, f32[512,512]{1,0:T(8,128)} %fock_hbm.1, f32[32]{0:T(128)} %ei_ref.1, f32[8]{0:T(128)} %ej_ref.1, f32[1,512]{1,0:T(1,128)} %bitcast.1), custom_call_target="tpu_custom_call" | custom-call | tf_op jit(solution)/shard_map/residual/pallas_call | solution.py:423
  122.1 2.3 %copy.8 = f32[1024,256]{1,0:T(8,128)} copy(f32[1024,256]{1,0:T(8,128)} %residual.1) | data formatting | bytes 2097152

commit v4 on v3

--- a/solution.py
+++ b/solution.py
@@ -350,8 +350,16 @@
         if 0 <= step - L3 < EVENTS:
             y_last(step - L3)
 
-    for h in range(2):
-        for part in range(2):
+    mine = pl.ds(pl.multiple_of(c * NB, NB), NB)
+    other = pl.ds(pl.multiple_of((1 - c) * NB, NB), NB)
+    nn, nt = ((1,), (0,)), ((1,), (1,))
+
+    def swap(part):
+        at = pl.ds(part * HM, HM)
+        return remote(racc.at[at, :], roth.at[at, :], cx.at[0, part], cx.at[1, part], partner)
+
+    for part in range(2):
+        for h in range(2):
             to_other(0, 0, part, h).wait_recv()
 
             def finish(i, _):
@@ -362,28 +370,22 @@
                 return 0
 
             lax.fori_loop(0, HM // 2 // CHUNK, finish, 0)
-
-    swap = remote(racc, roth, cx.at[0], cx.at[1], partner)
-    swap.start()
-
-    mine = pl.ds(pl.multiple_of(c * NB, NB), NB)
-    other = pl.ds(pl.multiple_of((1 - c) * NB, NB), NB)
-    nn, nt = ((1,), (0,)), ((1,), (1,))
-    for i in range(M // V):
-        at = pl.ds(i * V, V)
+        swap(part).start()
+        at = pl.ds(part * HM, HM)
         value = racc[at, :]
         parts = split(value)
         rows = value + dot3((fhi[...], flo[...]), parts, nn)
         out_ref[at, :] = rows + dot3(parts, (fhi[mine, mine], flo[mine, mine]), nt)
-    swap.wait_recv()
-    for i in range(M // V):
-        at = pl.ds(i * V, V)
+    for part in range(2):
+        swap(part).wait_recv()
+        at = pl.ds(part * HM, HM)
         parts = split(roth[at, :])
         out_ref[at, :] = (
             out_ref[at, :] + dot3(parts, (fhi[mine, other], flo[mine, other]), nt)
         ) * rec[at, :]
 
-    swap.wait_send()
+    for part in range(2):
+        swap(part).wait_send()
     w_swap.wait_send()
 
     @pl.when(jnp.logical_not(owner))
@@ -441,7 +443,7 @@
             pltpu.VMEM((V, V), BF16),
             dma((3,)), dma((2,)), dma((2,)), dma((EVENTS, 2)), dma((2, 6)), dma((2, 2, 2)),
             dma((8,)), dma((8, 2)), dma((EVENTS, 2, 2)),
-            dma((2, 2)), dma((2, 2)), dma((2,)),
+            dma((2, 2)), dma((2, 2)), dma((2, 2)),
         ],
         compiler_params=pltpu.CompilerParams(
             collective_id=0, has_side_effects=True, vmem_limit_bytes=60 * 1024 * 1024

time: 125 us -> 125 us (level)
  no operation moved by 1% of the time
where the time goes in v4:
time: 125 us
  Pallas kernels  122 us (98%)
  local copies, waits for them, and re-layouts  2.26 us (2%)
    pallas_call x1, Pallas kernels, per_device(): pl.pallas_call(kernel, out_shape=jax.ShapeDtypeStruct((M, NB), F32), in_s...  122 us

profile of v4, /device:TPU:193, one launch (start us, length us, event | category | flops | bytes accessed | tf_op | source)
XLA Modules:
  0.0 124.6 jit_solution(4313172266764735739)
XLA Ops:
  0.0 122.3 %residual.1 = f32[1024,256]{1,0:T(8,128)} custom-call(bf16[1024,1024]{1,0:T(8,128)(2,1)} %w_hbm.1, bf16[1024,256]{1,0:T(8,128)(2,1)} %a_hbm.1, f32[512,512]{1,0:T(8,128)} %fock_hbm.1, f32[32]{0:T(128)} %ei_ref.1, f32[8]{0:T(128)} %ej_ref.1, f32[1,512]{1,0:T(1,128)} %bitcast.1), custom_call_target="tpu_custom_call" | custom-call | tf_op jit(solution)/shard_map/residual/pallas_call | solution.py:425
  122.3 2.3 %copy.8 = f32[1024,256]{1,0:T(8,128)} copy(f32[1024,256]{1,0:T(8,128)} %residual.1) | data formatting | bytes 2097152
